TPU v7x, 32 devices: a whole 2x2x4 slice. The times are simulated.
32 devices in a mesh: patch: 8 (over z, y), coarse: 4 (over x, core).
Axes of the slice: x: 2, y: 2, z: 4, core: 2. Of those that a mesh axis runs over, the one named last changes fastest.
Arguments:
- residual: bfloat16 [2, 2, 49152, 256], P(None, None, ('patch', 'coarse')), may hold values from -6 to 6
- patch_inv: bfloat16 [128, 2, 1024, 1024], P(('patch', 'coarse')), may hold values from -0.1875 to 0.1875
- coarse_basis: bfloat16 [128, 2, 1024, 32], P(('patch', 'coarse')), may hold values from -0.1875 to 0.1875
- coarse_inv: bfloat16 [64, 2, 32, 32], P('coarse'), may hold values from -1 to 1
- patch_slots: int32 [128, 512], P(('patch', 'coarse')), may hold values from 0 to 1791, as said below
- send_rows: int32 [32, 2, 128], P(('patch', 'coarse')), may hold values from 0 to 1535, as said below
- coarse_block: int32 [128], P(('patch', 'coarse')), may hold values from 0 to 63
Outputs:
- correction: bfloat16 [2, 2, 49152, 256], P(None, None, ('patch', 'coarse'))
Inputs may be any that keep to these rules, and one draw needn't show every extreme that they name: `send_rows`: within each of the two blocks of a device the 128 rows are distinct. `patch_slots`: the 512 positions of a patch are distinct; they hold its device's rows (p mod 4) * 384 to (p mod 4 + 1) * 384 - 1, 64 positions of 1536 or more, and other rows of its device below 1536; each position of 1536 or more is used by exactly one patch of the device.
All inputs are finite; a program needn't handle non-finite values.
Results may differ from a plain program's by a relative error of at most 0.006.
Values may be sent and summed in bfloat16 or wider, within the bound.
No kernel may reach another device: no remote copies, remote signals or barrier semaphores. Data moves between devices by JAX's collectives and lax.ppermute only.
A program may use at most 128 MiB of HBM per device.

v0:
```python
import jax
import jax.numpy as jnp
from jax import lax
from jax.sharding import PartitionSpec as P


def passed_along(value, axis, steps):
    count = lax.axis_size(axis)
    pairs = [(source, (source + steps) % count) for source in range(count)]
    return lax.ppermute(value, axis, pairs)


def spread_rows(selector, terms, form):
    upper_part = terms.astype(jnp.bfloat16)
    lower_part = (terms - upper_part.astype(jnp.float32)).astype(jnp.bfloat16)
    first = jnp.einsum(form, selector, upper_part, preferred_element_type=jnp.float32)
    return first + jnp.einsum(form, selector, lower_part, preferred_element_type=jnp.float32)


def per_device(residual, patch_inv, coarse_basis, coarse_inv, patch_slots, send_rows, coarse_block):
    wave_count = residual.shape[0]
    node_rows = residual.shape[2]
    patches = patch_inv.shape[0]
    patch_nodes = patch_inv.shape[2] // 2
    coarse_width = coarse_basis.shape[3]
    slot_rows = send_rows.shape[2]
    ext_rows = node_rows + 2 * slot_rows
    blocks_all = coarse_inv.shape[0] * lax.axis_size("coarse")
    highest = lax.Precision.HIGHEST
    node_ids = jnp.arange(node_rows, dtype=jnp.int32)
    up_select = (send_rows[0, 0][:, None] == node_ids[None, :]).astype(jnp.bfloat16)
    down_select = (send_rows[0, 1][:, None] == node_ids[None, :]).astype(jnp.bfloat16)
    upward = jnp.einsum(
        "kn,wqnr->wqkr", up_select, residual, preferred_element_type=jnp.float32
    ).astype(jnp.bfloat16)
    downward = jnp.einsum(
        "kn,wqnr->wqkr", down_select, residual, preferred_element_type=jnp.float32
    ).astype(jnp.bfloat16)
    from_below = passed_along(upward, ("patch", "coarse"), 1)
    from_above = passed_along(downward, ("patch", "coarse"), -1)
    extended = jnp.concatenate([residual, from_below, from_above], axis=2)
    ext_select = (
        patch_slots[:, :, None] == jnp.arange(ext_rows, dtype=jnp.int32)[None, None, :]
    ).astype(jnp.bfloat16)
    gathered = jnp.einsum(
        "pne,wqer->wqpnr", ext_select, extended, preferred_element_type=jnp.float32
    ).astype(jnp.bfloat16)
    basis_cols = coarse_basis.reshape(patches, wave_count, 2, patch_nodes, coarse_width)
    restricted = jnp.einsum(
        "pwqnc,wqpnr->pwcr", basis_cols, gathered, preferred_element_type=jnp.float32
    )
    member = coarse_block[:, None] == jnp.arange(blocks_all, dtype=jnp.int32)[None, :]
    partial_sums = jnp.einsum(
        "pb,pwcr->bwcr", member.astype(jnp.float32), restricted, precision=highest
    )
    totals = lax.psum(partial_sums, ("patch", "coarse"))
    inverses = lax.all_gather(coarse_inv, "coarse", axis=0, tiled=True)
    coarse_coef = jnp.einsum(
        "bwcd,bwdr->bwcr", inverses.astype(jnp.float32), totals, precision=highest
    ).astype(jnp.bfloat16)
    patch_coef = jnp.einsum(
        "pb,bwcr->pwcr",
        member.astype(jnp.bfloat16),
        coarse_coef,
        preferred_element_type=jnp.float32,
    ).astype(jnp.bfloat16)
    inverse = patch_inv.reshape(patches, wave_count, 2, patch_nodes, 2, patch_nodes)
    local_terms = jnp.einsum(
        "pwabqn,wqpnr->wapbr", inverse, gathered, preferred_element_type=jnp.float32
    )
    local_terms = local_terms + jnp.einsum(
        "pwqnc,pwcr->wqpnr", basis_cols, patch_coef, preferred_element_type=jnp.float32
    )
    collected = spread_rows(ext_select, local_terms, "pne,wqpnr->wqer")
    to_lower = collected[:, :, node_rows : node_rows + slot_rows]
    to_upper = collected[:, :, node_rows + slot_rows :]
    back_from_above = passed_along(to_lower.astype(jnp.bfloat16), ("patch", "coarse"), -1).astype(
        to_lower.dtype
    )
    back_from_below = passed_along(to_upper.astype(jnp.bfloat16), ("patch", "coarse"), 1).astype(
        to_upper.dtype
    )
    summed = collected[:, :, :node_rows]
    summed = summed + spread_rows(up_select, back_from_above, "kn,wqkr->wqnr")
    summed = summed + spread_rows(down_select, back_from_below, "kn,wqkr->wqnr")
    return summed.astype(jnp.bfloat16)


def solution(mesh):
    placed = (
        P(None, None, ("patch", "coarse"), None),
        P(("patch", "coarse"), None, None, None),
        P(("patch", "coarse"), None, None, None),
        P("coarse", None, None, None),
        P(("patch", "coarse"), None),
        P(("patch", "coarse"), None, None),
        P(("patch", "coarse")),
    )
    return jax.shard_map(
        per_device,
        mesh=mesh,
        in_specs=placed,
        out_specs=P(None, None, ("patch", "coarse"), None),
        check_vma=False,
    )
```

profile of v0, /device:TPU:0, one launch (start us, length us, event | category | flops | bytes accessed | tf_op | source)
XLA Modules:
  0.0 256.1 jit_solution(5155626987619132174)
XLA Ops:
  6.5 0.0 copy-start
  6.5 0.0 all-reduce.2.cloned.1.call-start
  6.5 0.8 slice_bitcast_fusion.1
  7.4 2.6 %fusion.39 = bf16[2,2,128,256]{3,2,1,0:T(8,128)(2,1)S(1)} fusion(bf16[2,2,1536,256]{3,2,1,0:T(8,128)(2,1)} %param.7, s32[128]{0:T(128)S(1)} %get-tuple-element.7), kind=kOutput, calls=%fused_computation.37 | convolution fusion | flops 402980864 | bytes 3408384 | tf_op jit(solution)/shard_map/kn,wqnr->wqkr/dot_general | solution.py:33
  10.0 0.5 collective-permute-start
  10.6 3.2 %fusion.40 = bf16[2,2,128,256]{3,2,1,0:T(8,128)(2,1)} fusion(bf16[2,2,1536,256]{3,2,1,0:T(8,128)(2,1)} %param.7, s32[128]{0:T(128)S(1)} %get-tuple-element.8), kind=kOutput, calls=%fused_computation.38 | convolution fusion | flops 402980864 | bytes 3408384 | tf_op jit(solution)/shard_map/kn,wqnr->wqkr/dot_general | solution.py:36
  13.8 5.9 %collective-permute-start.1 = (bf16[2,2,128,256]{3,2,1,0:T(8,128)(2,1)}, bf16[2,2,128,256]{3,2,1,0:T(8,128)(2,1)}, u32[]{:S(2)}, u32[]{:S(2)}) collective-permute-start(bf16[2,2,128,256]{3,2,1,0:T(8,128)(2,1)} %fusion.40), channel_id=1, source_target_pairs={{0,31},{1,0},{2,1},{3,2},{4,3},{5,4},{6,5},{7,6},{8,7},{9,8},{10,9... | collective-permute-start | bytes 786440 | tf_op jit(solution)/shard_map/ppermute | solution.py:10
  19.7 0.0 copy-done
  19.7 2.8 %copy.22 = bf16[2,2,1536,256]{2,3,1,0:T(8,128)(2,1)} copy(bf16[2,2,1536,256]{3,2,1,0:T(8,128)(2,1)S(1)} %copy-done) | data formatting | bytes 6291456 | tf_op args[0]
  22.5 0.0 collective-permute-done
  22.5 1.1 copy.23
  23.6 0.3 collective-permute-done.1
  23.9 1.1 copy.24
  25.0 0.0 copy-done.5
  25.1 0.0 copy-start.2
  25.1 10.3 %fusion.29 = bf16[2,2,256,4,512]{4,2,3,1,0:T(8,128)(2,1)S(1)} fusion(s32[4,512]{1,0:T(4,128)S(1)} %copy-done.5, bf16[2,2,128,256]{2,3,1,0:T(8,128)(2,1)S(1)} %copy.24, bf16[2,2,128,256]{2,3,1,0:T(8,128)(2,1)S(1)} %copy.23, bf16[2,2,1536,256]{2,3,1,0:T(8,128)(2,1)} %copy.22), kind=kOutput, calls=%fused_computation.30 | convolution fusion | flops 7532969984 | bytes 7872512 | tf_op jit(solution)/shard_map/pne,wqer->wqpnr/dot_general | solution.py:45
  35.4 0.0 copy-start.6
  35.4 0.0 copy-start.4
  35.4 2.0 copy-done.6
  37.4 0.0 copy-done.2
  37.4 1.3 fusion.36
  38.7 0.0 copy-done.4
  38.8 3.9 %fusion.68 = f32[64,2,32,256]{3,0,2,1:T(8,128)} fusion(f32[4,2,32,256]{3,2,1,0:T(8,128)S(1)} %fusion.36, s32[4]{0:T(128)S(1)} %copy-done.4), kind=kOutput, calls=%fused_computation.60 | convolution fusion | flops 50331904 | bytes 4456464 | tf_op jit(solution)/shard_map/pb,pwcr->bwcr/dot_general | solution.py:53
  42.6 0.0 all-reduce.2.cloned.1.call-update
  42.7 0.4 reshape.11
  43.0 0.0 copy-start.3
  43.0 28.0 %reshape.10 = bf16[4,2,2,512,2,512]{5,4,3,2,1,0:T(2,128)(2,1)} reshape(bf16[4,2,1024,1024]{3,2,1,0:T(8,128)(2,1)} %param.8) | data formatting | bytes 33554432 | tf_op jit(solution)/shard_map/reshape | solution.py:67
  71.1 0.0 copy-done.3
  71.1 9.2 %all_gather.3 = bf16[64,2,32,32]{3,2,1,0:T(8,128)(2,1)S(1)} all-gather(bf16[16,2,32,32]{3,2,1,0:T(8,128)(2,1)S(1)} %copy-done.3), channel_id=1, replica_groups=mesh['patch'=8,'coarse'=4] {'coarse'}, dimensions={0}, use_global_device_ids=true | all-gather | bytes 327680 | tf_op jit(solution)/shard_map/all_gather | solution.py:57
  80.3 15.3 %fusion = f32[2,4,256,2,512,1]{4,2,5,3,1,0:T(8,128)} fusion(bf16[4,2,2,512,2,512]{5,4,3,2,1,0:T(2,128)(2,1)} %reshape.10, bf16[2,2,256,4,512]{4,2,3,1,0:T(8,128)(2,1)} %copy-done.6), kind=kOutput, calls=%fused_computation | convolution fusion | flops 4294967296 | bytes 29360128 | tf_op jit(solution)/shard_map/pwabqn,wqpnr->wapbr/dot_general | solution.py:68
  95.6 91.1 %all-reduce.2.cloned.1.call-done = f32[64,2,32,256]{3,0,2,1:T(8,128)} async-done(((f32[64,2,32,256]{3,0,2,1:T(8,128)}), f32[64,2,32,256]{3,0,2,1:T(8,128)}) %all-reduce.2.cloned.1.call-update) | async-done | bytes 4194320 | tf_op jit(solution)/shard_map/psum | solution.py:56
  186.7 7.1 %convert_bitcast_fusion = bf16[64,2,32,256]{3,2,1,0:T(8,128)(2,1)S(1)} fusion(bf16[64,2,32,32]{3,2,1,0:T(8,128)(2,1)S(1)} %all_gather.3, f32[64,2,32,256]{3,0,2,1:T(8,128)} %all-reduce.2.cloned.1.call-done), kind=kOutput, calls=%fused_computation.33 | convolution fusion | flops 403701760 | bytes 6553600 | tf_op jit(solution)/shard_map/bwcd,bwdr->bwcr/dot_general | solution.py:58
  193.8 1.2 fusion.44
  195.0 1.3 fusion.60
  196.3 0.0 copy-start.1
  196.3 3.2 %copy-done.1 = f32[2,4,256,2,512]{4,2,3,1,0:T(8,128)} copy-done((f32[2,4,256,2,512]{4,2,3,1,0:T(8,128)}, f32[2,4,256,2,512]{4,2,3,1,0:T(8,128)S(1)}, u32[]{:S(2)}) %copy-start.1) | copy-done | bytes 8388632
  199.5 13.1 %fusion.4 = f32[2,2,256,1792,1]{3,2,1,4,0:T(8,128)} fusion(s32[4,512]{1,0:T(4,128)S(1)} %copy-done.5, f32[2,4,256,2,512]{4,2,3,1,0:T(8,128)S(1)} %fusion.60, f32[2,4,256,2,512,1]{4,2,5,3,1,0:T(8,128)} %fusion), kind=kOutput, calls=%fused_computation.5 | convolution fusion | flops 7530348544 | bytes 24125440 | tf_op jit(solution)/shard_map/pne,wqpnr->wqer/dot_general | solution.py:17
  212.6 18.2 %fusion.78 = (bf16[2,2,1792,256]{2,3,1,0:T(8,128)(2,1)S(1)}, f32[2,2,1792,256]{2,3,1,0:T(8,128)}) fusion(f32[2,2,256,1792,1]{3,2,1,4,0:T(8,128)} %fusion.4, s32[4,512]{1,0:T(4,128)S(1)} %copy-done.5, f32[2,4,256,2,512]{4,2,3,1,0:T(8,128)} %copy-done.1, f32[2,4,256,2,512,1]{4,2,5,3,1,0:T(8,128)} %fusion), kind=kOutput, calls=%fused_computation.71 | convolution fusion | flops 7527727104 | bytes 35135488 | tf_op jit(solution)/shard_map/pne,wqpnr->wqer/dot_general | solution.py:16
  230.8 0.1 fusion.77
  230.9 0.9 collective-permute-start.2
  231.8 0.0 collective-permute-start.3
  231.8 3.9 %collective-permute-done.2 = bf16[2,2,128,256]{2,3,1,0:T(8,128)(2,1)S(1)} collective-permute-done((bf16[2,2,128,256]{2,3,1,0:T(8,128)(2,1)S(1)}, bf16[2,2,128,256]{2,3,1,0:T(8,128)(2,1)S(1)}, u32[]{:S(2)}, u32[]{:S(2)}) %collective-permute-start.2) | collective-permute-done | bytes 262176 | tf_op jit(solution)/shard_map/ppermute | solution.py:10
  235.7 1.1 fusion.48
  236.8 1.1 fusion.50
  237.9 3.3 %collective-permute-done.3 = bf16[2,2,128,256]{2,3,1,0:T(8,128)(2,1)S(1)} collective-permute-done((bf16[2,2,128,256]{2,3,1,0:T(8,128)(2,1)S(1)}, bf16[2,2,128,256]{2,3,1,0:T(8,128)(2,1)S(1)}, u32[]{:S(2)}, u32[]{:S(2)}) %collective-permute-start.3) | collective-permute-done | bytes 262176 | tf_op jit(solution)/shard_map/ppermute | solution.py:10
  241.2 1.1 fusion.54
  242.3 4.2 %fusion.16 = bf16[2,2,1536,256]{2,3,1,0:T(8,128)(2,1)S(1)} fusion(f32[2,2,1792,256]{2,3,1,0:T(8,128)} %get-tuple-element.10, f32[2,2,256,1536]{3,2,1,0:T(8,128)S(1)} %fusion.54, f32[2,2,256,1536]{3,2,1,0:T(8,128)S(1)} %fusion.50, f32[2,2,256,1536]{3,2,1,0:T(8,128)S(1)} %fusion.48, bf16[2,2,128,256]{2,3,1,0:T(8,128)(2,1)S(1)} %collective-permute-done.3, ...), kind=kOutput, calls=%fused_computation.19 | convolution fusion | flops 410714112 | bytes 28574208 | tf_op jit(solution)/shard_map/kn,wqkr->wqnr/dot_general | solution.py:16
  246.5 2.8 %copy.36 = bf16[2,2,1536,256]{3,2,1,0:T(8,128)(2,1)} copy(bf16[2,2,1536,256]{2,3,1,0:T(8,128)(2,1)S(1)} %fusion.16) | data formatting | bytes 6291456 | tf_op jit(solution)/shard_map/convert_element_type | solution.py:86
  (1 shorter events, 0.0 us)
Async XLA Ops:
  6.5 13.2 %copy-start = (bf16[2,2,1536,256]{3,2,1,0:T(8,128)(2,1)S(1)}, bf16[2,2,1536,256]{3,2,1,0:T(8,128)(2,1)}, u32[]{:S(2)}) copy-start(bf16[2,2,1536,256]{3,2,1,0:T(8,128)(2,1)} %param.7) | copy-start | bytes 9437188
  6.5 180.1 %all-reduce.2.cloned.1.call-start = ((), (), s32[]{:S(2)}) async-start(), calls=%async_computation | async-start | bytes 8388608 | tf_op jit(solution)/shard_map/psum | solution.py:56
  10.0 12.5 %collective-permute-start = (bf16[2,2,128,256]{3,2,1,0:T(8,128)(2,1)S(1)}, bf16[2,2,128,256]{3,2,1,0:T(8,128)(2,1)}, u32[]{:S(2)}, u32[]{:S(2)}) collective-permute-start(bf16[2,2,128,256]{3,2,1,0:T(8,128)(2,1)S(1)} %fusion.39), channel_id=1, source_target_pairs={{0,1},{1,2},{2,3},{3,4},{4,5},{5,6},{6,7},{7,8},{8,9},{9,10},{10,1... | collective-permute-start | bytes 786440 | tf_op jit(solution)/shard_map/ppermute | solution.py:10
  13.8 11.3 %copy-start.5 = (s32[4,512]{1,0:T(4,128)S(1)}, s32[4,512]{1,0:T(4,128)}, u32[]{:S(2)}) copy-start(s32[4,512]{1,0:T(4,128)} %param.11) | copy-start | bytes 24580
  13.8 10.1 %collective-permute-start.1 = (bf16[2,2,128,256]{3,2,1,0:T(8,128)(2,1)}, bf16[2,2,128,256]{3,2,1,0:T(8,128)(2,1)}, u32[]{:S(2)}, u32[]{:S(2)}) collective-permute-start(bf16[2,2,128,256]{3,2,1,0:T(8,128)(2,1)} %fusion.40), channel_id=1, source_target_pairs={{0,31},{1,0},{2,1},{3,2},{4,3},{5,4},{6,5},{7,6},{8,7},{9,8},{10,9... | collective-permute-start | bytes 786440 | tf_op jit(solution)/shard_map/ppermute | solution.py:10
  25.1 12.4 %copy-start.2 = (bf16[4,2,1024,32]{2,3,1,0:T(8,128)(2,1)S(1)}, bf16[4,2,1024,32]{2,3,1,0:T(8,128)(2,1)}, u32[]{:S(2)}) copy-start(bf16[4,2,1024,32]{2,3,1,0:T(8,128)(2,1)} %param.9) | copy-start | bytes 1572868
  35.4 2.1 copy-start.6
  35.4 3.4 %copy-start.4 = (s32[4]{0:T(128)S(1)}, s32[4]{0:T(128)}, u32[]{:S(2)}) copy-start(s32[4]{0:T(128)} %param.13) | copy-start | bytes 52
  43.0 28.0 %copy-start.3 = (bf16[16,2,32,32]{3,2,1,0:T(8,128)(2,1)S(1)}, bf16[16,2,32,32]{3,2,1,0:T(8,128)(2,1)}, u32[]{:S(2)}) copy-start(bf16[16,2,32,32]{3,2,1,0:T(8,128)(2,1)} %param.10) | copy-start | bytes 196612
  196.3 3.2 %copy-start.1 = (f32[2,4,256,2,512]{4,2,3,1,0:T(8,128)}, f32[2,4,256,2,512]{4,2,3,1,0:T(8,128)S(1)}, u32[]{:S(2)}) copy-start(f32[2,4,256,2,512]{4,2,3,1,0:T(8,128)S(1)} %fusion.60) | copy-start | bytes 25165828
  230.9 4.8 %collective-permute-start.2 = (bf16[2,2,128,256]{2,3,1,0:T(8,128)(2,1)S(1)}, bf16[2,2,128,256]{2,3,1,0:T(8,128)(2,1)S(1)}, u32[]{:S(2)}, u32[]{:S(2)}) collective-permute-start(bf16[2,2,128,256]{2,3,1,0:T(8,128)(2,1)S(1)} %get-tuple-element.5), channel_id=1, source_target_pairs={{0,31},{1,0},{2,1},{3,2},{4,3},{5,4},{6,5},{7,6},{8,7},{9,8},{10,9... | collective-permute-start | bytes 786440 | tf_op jit(solution)/shard_map/ppermute | solution.py:10
  231.8 9.4 %collective-permute-start.3 = (bf16[2,2,128,256]{2,3,1,0:T(8,128)(2,1)S(1)}, bf16[2,2,128,256]{2,3,1,0:T(8,128)(2,1)S(1)}, u32[]{:S(2)}, u32[]{:S(2)}) collective-permute-start(bf16[2,2,128,256]{2,3,1,0:T(8,128)(2,1)S(1)} %get-tuple-element.6), channel_id=1, source_target_pairs={{0,1},{1,2},{2,3},{3,4},{4,5},{5,6},{6,7},{7,8},{8,9},{9,10},{10,1... | collective-permute-start | bytes 786440 | tf_op jit(solution)/shard_map/ppermute | solution.py:10
Sparse Core Ops, SparseCore 0:
  42.8 143.8 all-reduce.1
where the time goes:
time: 257 us; the launch traced here: 256 us
  waiting for transfers between devices  98.6 us (38%)
  matrix products  84.9 us (33%)
  local copies, waits for them, and re-layouts  42.4 us (16%)
  between operations  13.5 us (5%)
  blocking collectives  9.23 us (4%)
  starting transfers between devices  7.39 us (3%)
    psum x1, waiting for transfers between devices, per_device(): totals = lax.psum(partial_sums, ('patch', 'coarse'))  91.1 us
    reshape x1, local copies, waits for them, and re-layouts, per_device(): patch_inv.reshape(patches, wave_count, 2, patch_nodes, 2, patch_nodes)  28 us
    dot_general x3, matrix products, spread_rows(): jnp.einsum(form, selector, upper_part, preferred_element_type=jnp.float32)  23.4 us
    dot_general x1, matrix products, per_device(): jnp.einsum('pwabqn,wqpnr->wapbr', inverse, gathered, preferred_element_ty...  15.3 us
    dot_general x3, matrix products, spread_rows(): jnp.einsum(form, selector, lower_part, preferred_element_type=jnp.float32)  15.3 us
    dot_general x1, matrix products, per_device(): jnp.einsum('pne,wqer->wqpnr', ext_select, extended, preferred_element_typ...  10.3 us
    all_gather x1, blocking collectives, per_device(): inverses = lax.all_gather(coarse_inv, 'coarse', axis=0, tiled=True)  9.23 us
    unnamed x15, local copies, waits for them, and re-layouts  8.05 us
  transfers between devices with their start and end apart: 5, of which 4 were waited for; matrix products, arithmetic and copies ran while one was open for 21% of the time, Pallas kernels for 0%

commit v1 on v0

--- a/solution.py
+++ b/solution.py
@@ -53,7 +53,9 @@
     partial_sums = jnp.einsum(
         "pb,pwcr->bwcr", member.astype(jnp.float32), restricted, precision=highest
     )
-    totals = lax.psum(partial_sums, ("patch", "coarse"))
+    totals = partial_sums
+    for name in ("coarse", "patch"):
+        totals = lax.psum(totals, name)
     inverses = lax.all_gather(coarse_inv, "coarse", axis=0, tiled=True)
     coarse_coef = jnp.einsum(
         "bwcd,bwdr->bwcr", inverses.astype(jnp.float32), totals, precision=highest

time: 257 us -> 362 us (1.41)
  waiting for transfers between devices: 98.6 us -> 202 us
    psum x1 -> x2, waiting for transfers between devices: 91.1 us -> 194 us  [per_device(): totals = lax.psum(totals, name)]
  transfers between devices with their start and end apart: 5 -> 6, of which waited for: 4 -> 5; matrix products, arithmetic and copies ran while one was open for 21% -> 15% of each run, Pallas kernels for 0% -> 0%
where the time goes in v1:
time: 362 us; the launch traced here: 361 us
  waiting for transfers between devices  202 us (56%)
  matrix products  84.8 us (23%)
  local copies, waits for them, and re-layouts  42.3 us (12%)
  between operations  13.5 us (4%)
  blocking collectives  9.41 us (3%)
  starting transfers between devices  9.1 us (3%)
    psum x2, waiting for transfers between devices, per_device(): totals = lax.psum(totals, name)  194 us
    reshape x1, local copies, waits for them, and re-layouts, per_device(): patch_inv.reshape(patches, wave_count, 2, patch_nodes, 2, patch_nodes)  28.1 us
    dot_general x3, matrix products, spread_rows(): jnp.einsum(form, selector, upper_part, preferred_element_type=jnp.float32)  23.4 us
    dot_general x3, matrix products, spread_rows(): jnp.einsum(form, selector, lower_part, preferred_element_type=jnp.float32)  15.3 us
    dot_general x1, matrix products, per_device(): jnp.einsum('pwabqn,wqpnr->wapbr', inverse, gathered, preferred_element_ty...  15.2 us
    dot_general x1, matrix products, per_device(): jnp.einsum('pne,wqer->wqpnr', ext_select, extended, preferred_element_typ...  10.3 us
    all_gather x1, blocking collectives, per_device(): inverses = lax.all_gather(coarse_inv, 'coarse', axis=0, tiled=True)  9.41 us
    ppermute x4, starting transfers between devices, passed_along(): return lax.ppermute(value, axis, pairs)  9.06 us
  transfers between devices with their start and end apart: 6, of which 5 were waited for; matrix products, arithmetic and copies ran while one was open for 15% of the time, Pallas kernels for 0%

profile of v1, /device:TPU:0, one launch (start us, length us, event | category | flops | bytes accessed | tf_op | source)
XLA Modules:
  0.0 360.8 jit_solution(7779572696223923256)
XLA Ops:
  6.5 0.0 all-reduce.3.cloned.1.call-start
  6.5 0.8 slice_bitcast_fusion.1
  7.4 2.6 fusion.39
  10.0 0.5 collective-permute-start
  10.6 3.2 fusion.40
  13.8 5.9 %collective-permute-start.1 = (bf16[2,2,128,256]{3,2,1,0:T(8,128)(2,1)}, bf16[2,2,128,256]{3,2,1,0:T(8,128)(2,1)}, u32[]{:S(2)}, u32[]{:S(2)}) collective-permute-start(bf16[2,2,128,256]{3,2,1,0:T(8,128)(2,1)} %fusion.40), channel_id=1, source_target_pairs={{0,31},{1,0},{2,1},{3,2},{4,3},{5,4},{6,5},{7,6},{8,7},{9,8},{10,9... | collective-permute-start | bytes 786440 | tf_op jit(solution)/shard_map/ppermute | solution.py:10
  19.7 0.0 copy-done
  19.7 2.8 copy.22
  22.5 0.0 collective-permute-done
  22.5 1.1 copy.23
  23.6 0.3 collective-permute-done.1
  23.9 1.1 copy.24
  25.0 0.0 copy-done.5
  25.1 0.0 copy-start.2
  25.1 10.3 %fusion.29 = bf16[2,2,256,4,512]{4,2,3,1,0:T(8,128)(2,1)S(1)} fusion(s32[4,512]{1,0:T(4,128)S(1)} %copy-done.5, bf16[2,2,128,256]{2,3,1,0:T(8,128)(2,1)S(1)} %copy.24, bf16[2,2,128,256]{2,3,1,0:T(8,128)(2,1)S(1)} %copy.23, bf16[2,2,1536,256]{2,3,1,0:T(8,128)(2,1)} %copy.22), kind=kOutput, calls=%fused_computation.30 | convolution fusion | flops 7532969984 | bytes 7872512 | tf_op jit(solution)/shard_map/pne,wqer->wqpnr/dot_general | solution.py:45
  35.4 0.0 copy-start.6
  35.4 0.0 copy-start.4
  35.4 1.9 copy-done.6
  37.3 0.0 copy-done.2
  37.3 1.3 fusion.36
  38.6 0.0 copy-done.4
  38.6 3.9 %fusion.68 = f32[64,2,32,256]{3,0,2,1:T(8,128)} fusion(f32[4,2,32,256]{3,2,1,0:T(8,128)S(1)} %fusion.36, s32[4]{0:T(128)S(1)} %copy-done.4), kind=kOutput, calls=%fused_computation.60 | convolution fusion | flops 50331904 | bytes 4456464 | tf_op jit(solution)/shard_map/pb,pwcr->bwcr/dot_general | solution.py:53
  42.5 0.0 all-reduce.3.cloned.1.call-update
  42.5 0.0 all-reduce.5.cloned.1.call-start
  42.6 86.9 %all-reduce.3.cloned.1.call-done = f32[64,2,32,256]{3,0,2,1:T(8,128)} async-done(((f32[64,2,32,256]{3,0,2,1:T(8,128)}), f32[64,2,32,256]{3,0,2,1:T(8,128)}) %all-reduce.3.cloned.1.call-update) | async-done | bytes 4194320 | tf_op jit(solution)/shard_map/psum | solution.py:58
  129.5 0.0 all-reduce.5.cloned.1.call-update
  129.5 0.4 reshape.11
  129.9 0.0 copy-start.3
  129.9 28.1 %reshape.10 = bf16[4,2,2,512,2,512]{5,4,3,2,1,0:T(2,128)(2,1)} reshape(bf16[4,2,1024,1024]{3,2,1,0:T(8,128)(2,1)} %param.8) | data formatting | bytes 33554432 | tf_op jit(solution)/shard_map/reshape | solution.py:69
  158.0 9.4 %all_gather.3 = bf16[64,2,32,32]{3,2,1,0:T(8,128)(2,1)S(1)} all-gather(bf16[16,2,32,32]{3,2,1,0:T(8,128)(2,1)S(1)} %copy-done.3), channel_id=1, replica_groups=mesh['patch'=8,'coarse'=4] {'coarse'}, dimensions={0}, use_global_device_ids=true | all-gather | bytes 327680 | tf_op jit(solution)/shard_map/all_gather | solution.py:59
  167.4 15.2 %fusion = f32[2,4,256,2,512,1]{4,2,5,3,1,0:T(8,128)} fusion(bf16[4,2,2,512,2,512]{5,4,3,2,1,0:T(2,128)(2,1)} %reshape.10, bf16[2,2,256,4,512]{4,2,3,1,0:T(8,128)(2,1)} %copy-done.6), kind=kOutput, calls=%fused_computation | convolution fusion | flops 4294967296 | bytes 29360128 | tf_op jit(solution)/shard_map/pwabqn,wqpnr->wapbr/dot_general | solution.py:70
  182.6 107.2 %all-reduce.5.cloned.1.call-done = f32[64,2,32,256]{3,0,2,1:T(8,128)} async-done(((f32[64,2,32,256]{3,0,2,1:T(8,128)}), f32[64,2,32,256]{3,0,2,1:T(8,128)}) %all-reduce.5.cloned.1.call-update) | async-done | bytes 4194320 | tf_op jit(solution)/shard_map/psum | solution.py:58
  289.8 7.1 %convert_bitcast_fusion = bf16[64,2,32,256]{3,2,1,0:T(8,128)(2,1)S(1)} fusion(bf16[64,2,32,32]{3,2,1,0:T(8,128)(2,1)S(1)} %all_gather.3, f32[64,2,32,256]{3,0,2,1:T(8,128)} %all-reduce.5.cloned.1.call-done), kind=kOutput, calls=%fused_computation.33 | convolution fusion | flops 403701760 | bytes 6553600 | tf_op jit(solution)/shard_map/bwcd,bwdr->bwcr/dot_general | solution.py:60
  296.9 1.2 fusion.44
  298.1 1.3 fusion.60
  299.4 3.2 copy-done.1
  302.6 13.1 %fusion.4 = f32[2,2,256,1792,1]{3,2,1,4,0:T(8,128)} fusion(s32[4,512]{1,0:T(4,128)S(1)} %copy-done.5, f32[2,4,256,2,512]{4,2,3,1,0:T(8,128)S(1)} %fusion.60, f32[2,4,256,2,512,1]{4,2,5,3,1,0:T(8,128)} %fusion), kind=kOutput, calls=%fused_computation.5 | convolution fusion | flops 7530348544 | bytes 24125440 | tf_op jit(solution)/shard_map/pne,wqpnr->wqer/dot_general | solution.py:17
  315.7 18.2 %fusion.78 = (bf16[2,2,1792,256]{2,3,1,0:T(8,128)(2,1)S(1)}, f32[2,2,1792,256]{2,3,1,0:T(8,128)}) fusion(f32[2,2,256,1792,1]{3,2,1,4,0:T(8,128)} %fusion.4, s32[4,512]{1,0:T(4,128)S(1)} %copy-done.5, f32[2,4,256,2,512]{4,2,3,1,0:T(8,128)} %copy-done.1, f32[2,4,256,2,512,1]{4,2,5,3,1,0:T(8,128)} %fusion), kind=kOutput, calls=%fused_computation.71 | convolution fusion | flops 7527727104 | bytes 35135488 | tf_op jit(solution)/shard_map/pne,wqpnr->wqer/dot_general | solution.py:16
  333.9 0.1 fusion.77
  334.0 2.6 collective-permute-start.2
  336.6 0.0 collective-permute-start.3
  336.6 3.9 %collective-permute-done.2 = bf16[2,2,128,256]{2,3,1,0:T(8,128)(2,1)S(1)} collective-permute-done((bf16[2,2,128,256]{2,3,1,0:T(8,128)(2,1)S(1)}, bf16[2,2,128,256]{2,3,1,0:T(8,128)(2,1)S(1)}, u32[]{:S(2)}, u32[]{:S(2)}) %collective-permute-start.2) | collective-permute-done | bytes 262176 | tf_op jit(solution)/shard_map/ppermute | solution.py:10
  340.5 1.1 fusion.48
  341.6 1.1 fusion.50
  342.6 3.3 collective-permute-done.3
  346.0 1.1 fusion.54
  347.1 4.2 %fusion.16 = bf16[2,2,1536,256]{2,3,1,0:T(8,128)(2,1)S(1)} fusion(f32[2,2,1792,256]{2,3,1,0:T(8,128)} %get-tuple-element.10, f32[2,2,256,1536]{3,2,1,0:T(8,128)S(1)} %fusion.54, f32[2,2,256,1536]{3,2,1,0:T(8,128)S(1)} %fusion.50, f32[2,2,256,1536]{3,2,1,0:T(8,128)S(1)} %fusion.48, bf16[2,2,128,256]{2,3,1,0:T(8,128)(2,1)S(1)} %collective-permute-done.3, ...), kind=kOutput, calls=%fused_computation.19 | convolution fusion | flops 410714112 | bytes 28574208 | tf_op jit(solution)/shard_map/kn,wqkr->wqnr/dot_general | solution.py:16
  351.2 2.8 copy.36
  (4 shorter events, 0.0 us)
Async XLA Ops:
  6.5 13.2 %copy-start = (bf16[2,2,1536,256]{3,2,1,0:T(8,128)(2,1)S(1)}, bf16[2,2,1536,256]{3,2,1,0:T(8,128)(2,1)}, u32[]{:S(2)}) copy-start(bf16[2,2,1536,256]{3,2,1,0:T(8,128)(2,1)} %param.7) | copy-start | bytes 9437188
  6.5 123.0 %all-reduce.3.cloned.1.call-start = ((), (), s32[]{:S(2)}) async-start(), calls=%async_computation | async-start | bytes 8388608 | tf_op jit(solution)/shard_map/psum | solution.py:58
  10.0 12.5 %collective-permute-start = (bf16[2,2,128,256]{3,2,1,0:T(8,128)(2,1)S(1)}, bf16[2,2,128,256]{3,2,1,0:T(8,128)(2,1)}, u32[]{:S(2)}, u32[]{:S(2)}) collective-permute-start(bf16[2,2,128,256]{3,2,1,0:T(8,128)(2,1)S(1)} %fusion.39), channel_id=1, source_target_pairs={{0,1},{1,2},{2,3},{3,4},{4,5},{5,6},{6,7},{7,8},{8,9},{9,10},{10,1... | collective-permute-start | bytes 786440 | tf_op jit(solution)/shard_map/ppermute | solution.py:10
  13.8 11.3 %copy-start.5 = (s32[4,512]{1,0:T(4,128)S(1)}, s32[4,512]{1,0:T(4,128)}, u32[]{:S(2)}) copy-start(s32[4,512]{1,0:T(4,128)} %param.11) | copy-start | bytes 24580
  13.8 10.1 %collective-permute-start.1 = (bf16[2,2,128,256]{3,2,1,0:T(8,128)(2,1)}, bf16[2,2,128,256]{3,2,1,0:T(8,128)(2,1)}, u32[]{:S(2)}, u32[]{:S(2)}) collective-permute-start(bf16[2,2,128,256]{3,2,1,0:T(8,128)(2,1)} %fusion.40), channel_id=1, source_target_pairs={{0,31},{1,0},{2,1},{3,2},{4,3},{5,4},{6,5},{7,6},{8,7},{9,8},{10,9... | collective-permute-start | bytes 786440 | tf_op jit(solution)/shard_map/ppermute | solution.py:10
  25.1 12.3 %copy-start.2 = (bf16[4,2,1024,32]{2,3,1,0:T(8,128)(2,1)S(1)}, bf16[4,2,1024,32]{2,3,1,0:T(8,128)(2,1)}, u32[]{:S(2)}) copy-start(bf16[4,2,1024,32]{2,3,1,0:T(8,128)(2,1)} %param.9) | copy-start | bytes 1572868
  35.4 1.9 copy-start.6
  35.4 3.2 copy-start.4
  42.5 247.2 %all-reduce.5.cloned.1.call-start = ((), (), s32[]{:S(2)}) async-start(), calls=%async_computation.1 | async-start | bytes 8388608 | tf_op jit(solution)/shard_map/psum | solution.py:58
  129.9 28.1 %copy-start.3 = (bf16[16,2,32,32]{3,2,1,0:T(8,128)(2,1)S(1)}, bf16[16,2,32,32]{3,2,1,0:T(8,128)(2,1)}, u32[]{:S(2)}) copy-start(bf16[16,2,32,32]{3,2,1,0:T(8,128)(2,1)} %param.10) | copy-start | bytes 196612
  299.4 3.2 copy-start.1
  334.0 6.5 %collective-permute-start.2 = (bf16[2,2,128,256]{2,3,1,0:T(8,128)(2,1)S(1)}, bf16[2,2,128,256]{2,3,1,0:T(8,128)(2,1)S(1)}, u32[]{:S(2)}, u32[]{:S(2)}) collective-permute-start(bf16[2,2,128,256]{2,3,1,0:T(8,128)(2,1)S(1)} %get-tuple-element.5), channel_id=1, source_target_pairs={{0,31},{1,0},{2,1},{3,2},{4,3},{5,4},{6,5},{7,6},{8,7},{9,8},{10,9... | collective-permute-start | bytes 786440 | tf_op jit(solution)/shard_map/ppermute | solution.py:10
  336.6 9.4 %collective-permute-start.3 = (bf16[2,2,128,256]{2,3,1,0:T(8,128)(2,1)S(1)}, bf16[2,2,128,256]{2,3,1,0:T(8,128)(2,1)S(1)}, u32[]{:S(2)}, u32[]{:S(2)}) collective-permute-start(bf16[2,2,128,256]{2,3,1,0:T(8,128)(2,1)S(1)} %get-tuple-element.6), channel_id=1, source_target_pairs={{0,1},{1,2},{2,3},{3,4},{4,5},{5,6},{6,7},{7,8},{8,9},{9,10},{10,1... | collective-permute-start | bytes 786440 | tf_op jit(solution)/shard_map/ppermute | solution.py:10
Sparse Core Ops, SparseCore 0:
  42.7 86.7 all-reduce.2
  133.2 156.5 all-reduce.4
